TPU v7x, 128 devices: a whole 4x4x4 slice. The times are simulated.
128 devices in a mesh: req: 16 (over z, y), kv: 8 (over x, core).
Axes of the slice: x: 4, y: 4, z: 4, core: 2. Of those that a mesh axis runs over, the one named last changes fastest.
Arguments:
- hidden_in: bfloat16 [16384, 2048], P(('req', 'kv')), may hold values from -6 to 6
- slot_tokens: int32 [16384], replicated, may hold values from 0 to 16383, as said below
- cache_len: int32 [128], P('req'), may hold values from 1 to 2048, 65536 in all
- prefill_start: int32 [16], P('req'), may hold values from 0 to 2048
- key_cache: bfloat16 [128, 2048, 1024], P('req', None, 'kv')
- value_cache: bfloat16 [128, 2048, 1024], P('req', None, 'kv'), may hold values from -18 to 18
- key_prefix: bfloat16 [16, 2048, 1024], P('req', None, 'kv')
- value_prefix: bfloat16 [16, 2048, 1024], P('req', None, 'kv'), may hold values from -18 to 18
- attn_gain: float32 [2048], replicated, may hold values from 0.25 to 1.75
- q_proj: bfloat16 [2048, 2048], P(None, 'kv'), may hold values from -0.125 to 0.125
- k_proj: bfloat16 [2048, 1024], P(None, 'kv'), may hold values from -0.125 to 0.125
- v_proj: bfloat16 [2048, 1024], P(None, 'kv'), may hold values from -0.125 to 0.125
- q_gain: float32 [128], replicated, may hold values from 0.25 to 1.75
- k_gain: float32 [128], replicated, may hold values from 0.25 to 1.75
- o_proj: bfloat16 [2048, 2048], P('kv'), may hold values from -0.125 to 0.125
- ffn_gain: float32 [2048], replicated, may hold values from 0.25 to 1.75
- w_gate: bfloat16 [2048, 6144], P(None, 'req'), may hold values from -0.125 to 0.125
- w_up: bfloat16 [2048, 6144], P(None, 'req'), may hold values from -0.125 to 0.125
- w_down: bfloat16 [6144, 2048], P('req'), may hold values from -0.078125 to 0.078125
- final_gain: float32 [2048], replicated, may hold values from 0.25 to 1.75
- lm_head: bfloat16 [2048, 151936], P(None, ('req', 'kv')), may hold values from -0.375 to 0.375
Outputs:
- layer_out: bfloat16 [16384, 2048], P(('req', 'kv'))
- max_logit: float32 [144], replicated
Inputs may be any that keep to these rules, and one draw needn't show every extreme that they name: slot_tokens is a permutation of the batch's tokens; each device's 128 consecutive slots take exactly 1 token from each device's 128 consecutive batch tokens.
All inputs are finite; a program needn't handle non-finite values. No bound on the sum of `cache_len` on one device may be relied on, other than what follows from the above.
Results may differ from a plain program's by a relative error of at most 0.0085.
The roundings to bfloat16 on the way count: a program that leaves them out, or rounds other values in their place, can miss the bound.
Values may be sent and summed in bfloat16 or wider, within the bound.
A program may use at most 128 MiB of HBM per device.

v0:
```python
import jax
import jax.numpy as jnp
from jax import lax
from jax.sharding import PartitionSpec as P

EPS = 1e-06
NEG = -1e30


def spread(value, axis, root):
    mine = lax.axis_index(axis) == root
    return lax.psum(jnp.where(mine, value, jnp.zeros_like(value)), axis)


def norm_rows(values, gain_vec):
    wide = values.astype(jnp.float32)
    return wide * lax.rsqrt(jnp.mean(wide * wide, axis=-1, keepdims=True) + EPS) * gain_vec


def rotate(values, places):
    half_dim = values.shape[-1] // 2
    freqs = 1000000.0 ** (-(jnp.arange(half_dim, dtype=jnp.float32) * 2.0 / values.shape[-1]))
    angles = places[:, None] * freqs[None, :]
    cosine = jnp.cos(angles)[:, None, :]
    sine = jnp.sin(angles)[:, None, :]
    first_half = values[..., :half_dim]
    second_half = values[..., half_dim:]
    return jnp.concatenate(
        [first_half * cosine - second_half * sine, second_half * cosine + first_half * sine],
        axis=-1,
    )


def prefill_full(q_heads, key_old, value_old, key_new, value_new, start_at):
    old_len = key_old.shape[0]
    fresh_rows = q_heads.shape[0]
    factor = q_heads.shape[-1] ** (-0.5)
    all_keys = jnp.concatenate([key_old, key_new], axis=0)
    all_values = jnp.concatenate([value_old, value_new], axis=0)
    scores = (
        jnp.einsum("cgd,kd->gck", q_heads, all_keys, preferred_element_type=jnp.float32) * factor
    )
    key_index = jnp.arange(old_len + fresh_rows, dtype=jnp.int32)[None, :]
    row_index = jnp.arange(fresh_rows, dtype=jnp.int32)[:, None]
    allowed = jnp.where(key_index < old_len, key_index < start_at, key_index - old_len <= row_index)
    scores = jnp.where(allowed[None], scores, NEG)
    row_peak = jnp.max(scores, axis=-1, keepdims=True)
    expd = jnp.exp(scores - row_peak)
    weights = (expd / jnp.sum(expd, axis=-1, keepdims=True)).astype(jnp.bfloat16)
    return jnp.einsum(
        "gck,kd->cgd", weights, all_values, preferred_element_type=jnp.float32
    ).astype(jnp.bfloat16)


def decode_attend(q_heads, key_old, value_old, key_self, value_self, lengths):
    factor = q_heads.shape[-1] ** (-0.5)
    past = jnp.einsum("bgd,bld->bgl", q_heads, key_old, preferred_element_type=jnp.float32) * factor
    slot_index = jnp.arange(key_old.shape[1], dtype=jnp.int32)
    past = jnp.where(slot_index[None, None, :] < lengths[:, None, None], past, NEG)
    own_score = (
        jnp.einsum("bgd,bd->bg", q_heads, key_self, preferred_element_type=jnp.float32) * factor
    )
    row_peak = jnp.maximum(jnp.max(past, axis=-1), own_score)
    past_exp = jnp.exp(past - row_peak[..., None])
    own_exp = jnp.exp(own_score - row_peak)
    row_total = jnp.sum(past_exp, axis=-1) + own_exp
    past_w = (past_exp / row_total[..., None]).astype(jnp.bfloat16)
    own_w = (own_exp / row_total).astype(jnp.bfloat16)
    summed = jnp.einsum("bgl,bld->bgd", past_w, value_old, preferred_element_type=jnp.float32)
    summed = (
        summed + own_w.astype(jnp.float32)[..., None] * value_self.astype(jnp.float32)[:, None, :]
    )
    return summed.astype(jnp.bfloat16)


def regroup(rows_in):
    return lax.all_to_all(rows_in, ("req", "kv"), split_axis=0, concat_axis=0, tiled=True)


def shards(
    hidden_in,
    slot_tokens,
    cache_len,
    prefill_start,
    key_cache,
    value_cache,
    key_prefix,
    value_prefix,
    attn_gain,
    q_proj,
    k_proj,
    v_proj,
    q_gain,
    k_gain,
    o_proj,
    ffn_gain,
    w_gate,
    w_up,
    w_down,
    final_gain,
    lm_head,
):
    req_count = lax.axis_size("req")
    kv_count = lax.axis_size("kv")
    devices = req_count * kv_count
    rows_dev = hidden_in.shape[0]
    per_pair = rows_dev // devices
    self_index = lax.axis_index("req") * kv_count + lax.axis_index("kv")
    slot_table = slot_tokens.reshape(devices, rows_dev)
    from_self = slot_table // rows_dev == self_index
    picked = jnp.argsort(jnp.where(from_self, 0, 1).astype(jnp.int32), axis=1, stable=True)[
        :, :per_pair
    ]
    send_rows = (jnp.take_along_axis(slot_table, picked, axis=1) - self_index * rows_dev).reshape(
        -1
    )
    own_sources = lax.dynamic_index_in_dim(slot_table, self_index, 0, keepdims=False) // rows_dev
    marks = (own_sources[:, None] == jnp.arange(devices, dtype=jnp.int32)[None, :]).astype(
        jnp.int32
    )
    ranks = jnp.sum(marks * (jnp.cumsum(marks, axis=0) - 1), axis=1)
    slot_place = own_sources * per_pair + ranks
    arrived = regroup(hidden_in[send_rows])
    owner_rows = arrived[slot_place]
    normed = norm_rows(owner_rows, attn_gain).astype(jnp.bfloat16)
    q_cols = q_proj.shape[1]
    kv_cols = k_proj.shape[1]
    rows_piece = lax.all_gather(normed, "kv", axis=0, tiled=True)
    projected = jnp.concatenate(
        [
            jnp.dot(rows_piece, q_proj, preferred_element_type=jnp.float32),
            jnp.dot(rows_piece, k_proj, preferred_element_type=jnp.float32),
            jnp.dot(rows_piece, v_proj, preferred_element_type=jnp.float32),
        ],
        axis=1,
    )
    tok_req = projected.shape[0]
    head_dim = q_gain.shape[0]
    dec_count = cache_len.shape[0]
    fresh_count = tok_req - dec_count
    q_raw = projected[:, :q_cols].reshape(tok_req, q_cols // head_dim, head_dim)
    k_raw = projected[:, q_cols : q_cols + kv_cols].reshape(tok_req, kv_cols // head_dim, head_dim)
    v_new = (
        projected[:, q_cols + kv_cols :]
        .astype(jnp.bfloat16)
        .reshape(tok_req, kv_cols // head_dim, head_dim)
    )
    places = jnp.concatenate(
        [prefill_start[0] + jnp.arange(fresh_count, dtype=jnp.int32), cache_len]
    ).astype(jnp.float32)
    queries = rotate(norm_rows(q_raw, q_gain), places).astype(jnp.bfloat16)
    keys_new = rotate(norm_rows(k_raw, k_gain), places).astype(jnp.bfloat16)
    pre_out = prefill_full(
        queries[:fresh_count],
        key_prefix[0, :, 0:head_dim],
        value_prefix[0, :, 0:head_dim],
        keys_new[:fresh_count, 0],
        v_new[:fresh_count, 0],
        prefill_start[0],
    )
    dec_out = decode_attend(
        queries[fresh_count:],
        key_cache,
        value_cache,
        keys_new[fresh_count:, 0],
        v_new[fresh_count:, 0],
        cache_len,
    )
    pieces = jnp.concatenate([pre_out, dec_out], axis=0)
    attended = pieces.reshape(tok_req, q_cols)
    attn_part = lax.psum_scatter(
        jnp.dot(attended, o_proj, preferred_element_type=jnp.float32),
        "kv",
        scatter_dimension=0,
        tiled=True,
    )
    resid = (owner_rows.astype(jnp.float32) + attn_part).astype(jnp.bfloat16)
    ffn_in = norm_rows(resid, ffn_gain).astype(jnp.bfloat16)
    rows_piece = lax.all_gather(ffn_in, "req", axis=0, tiled=True)
    gate_part = jnp.dot(rows_piece, w_gate, preferred_element_type=jnp.float32)
    up_part = jnp.dot(rows_piece, w_up, preferred_element_type=jnp.float32)
    hidden_act = (jax.nn.silu(gate_part) * up_part).astype(jnp.bfloat16)
    ffn_part = lax.psum_scatter(
        jnp.dot(hidden_act, w_down, preferred_element_type=jnp.float32),
        "req",
        scatter_dimension=0,
        tiled=True,
    )
    out_rows = (resid.astype(jnp.float32) + ffn_part).astype(jnp.bfloat16)
    going_back = jnp.zeros_like(out_rows).at[slot_place].set(out_rows)
    returned = regroup(going_back)
    layer_out = jnp.zeros_like(hidden_in).at[send_rows].set(returned)
    tail_rows = norm_rows(out_rows[rows_dev - dec_count - 1 :], final_gain).astype(jnp.bfloat16)
    tail_rows = spread(tail_rows, "kv", kv_count - 1)
    local_peaks = jnp.max(
        jnp.dot(
            lax.all_gather(tail_rows, "req", axis=0, tiled=True),
            lm_head,
            preferred_element_type=jnp.float32,
        ),
        axis=1,
    )
    max_logit = lax.pmax(local_peaks, ("req", "kv"))
    return (layer_out, max_logit)


def solution(mesh):
    placed = (
        P(("req", "kv"), None),
        P(),
        P("req"),
        P("req"),
        P("req", None, "kv"),
        P("req", None, "kv"),
        P("req", None, "kv"),
        P("req", None, "kv"),
        P(),
        P(None, "kv"),
        P(None, "kv"),
        P(None, "kv"),
        P(),
        P(),
        P("kv", None),
        P(),
        P(None, "req"),
        P(None, "req"),
        P("req", None),
        P(),
        P(None, ("req", "kv")),
    )
    return jax.shard_map(
        shards, mesh=mesh, in_specs=placed, out_specs=(P(("req", "kv"), None), P()), check_vma=False
    )
```

profile of v0, /device:TPU:1, one launch (start us, length us, event | category | flops | bytes accessed | tf_op | source)
XLA Modules:
  0.0 540.3 jit_solution(2482450521483599496)
XLA Ops:
  7.2 1.7 fusion.60
  11.1 4.7 sort.19.cloned.1.call-done
  17.0 1.9 gather_fusion.2
  23.6 11.5 %all-to-all-start = ((bf16[128,2,1024]{2,1,0:T(2,128)(2,1)}), bf16[128,2,1024]{2,1,0:T(2,128)(2,1)S(1)}, u32[]{:S(2)}, u32[]{:S(2)}) async-start(bf16[128,2,1024]{2,1,0:T(2,128)(2,1)} %reshape.484), calls=%async_computation | async-start | bytes 1048576 | tf_op jit(solution)/shard_map/all_to_all | solution.py:77
  35.9 13.0 %all-to-all-done = bf16[128,2,1024]{2,1,0:T(2,128)(2,1)S(1)} async-done(((bf16[128,2,1024]{2,1,0:T(2,128)(2,1)}), bf16[128,2,1024]{2,1,0:T(2,128)(2,1)S(1)}, u32[]{:S(2)}, u32[]{:S(2)}) %all-to-all-start) | async-done | bytes 524320 | tf_op jit(solution)/shard_map/all_to_all | solution.py:77
  48.9 1.7 reshape.485
  50.6 1.5 copy.105
  55.4 3.1 multiply_cosine_fusion
  58.6 4.2 fusion.4
  62.7 20.4 %all-gather.4.cloned.1.call-done = bf16[1024,2048]{1,0:T(8,128)(2,1)} async-done(((bf16[128,2048]{1,0:T(8,128)(2,1)}), bf16[1024,2048]{1,0:T(8,128)(2,1)}) %all-gather.4.cloned.1.call-update) | async-done | bytes 4194320 | tf_op jit(solution)/shard_map/all_gather | solution.py:128
  83.2 3.6 convolution_convert_fusion
  87.5 1.5 multiply_reduce_fusion.1
  90.5 2.3 multiply_reduce_fusion
  92.8 1.5 copy.81
  95.7 1.8 subtract_convert_fusion
  99.4 2.9 fusion.43
  102.4 15.9 %fusion.84 = (f32[2,1016]{1,0:T(2,128)S(1)}, f32[2,1016,3064]{2,1,0:T(8,128)}) fusion(pred[1016,3064]{1,0:T(8,128)(4,1)} %fusion.4, bf16[1016,128]{1,0:T(8,128)(2,1)} %copy.80, bf16[2048,128]{1,0:T(8,128)(2,1)} %bitcast.105, bf16[1024,2,64]{2,0,1:T(8,128)(2,1)S(1)} %get-tuple-element.6, bf16[1024,2,64]{2,0,1:T(8,128)(2,1)S(1)} %get-tuple-element.7), kind=kOutput, calls=%fused_computation.161 | convolution fusion | flops 1621384704 | bytes 29334016 | tf_op jit(solution)/shard_map/sub | solution.py:48
  118.3 11.7 %fusion.12 = bf16[1016,2,128]{2,0,1:T(8,128)(2,1)S(1)} fusion(f32[2,1016,3064]{2,1,0:T(8,128)} %get-tuple-element.21, f32[2,1016]{1,0:T(2,128)S(1)} %get-tuple-element.20, bf16[1016,128]{1,0:T(8,128)(2,1)S(1)} %copy-done.5, bf16[2048,128]{1,0:T(8,128)(2,1)} %bitcast.106), kind=kOutput, calls=%fused_computation.28 | convolution fusion | flops 1608149248 | bytes 26216896 | tf_op jit(solution)/shard_map/gck,kd->cgd/dot_general | solution.py:50
  130.3 5.7 %fusion.89 = f32[1024,2048]{1,0:T(8,128)} fusion(bf16[1024,256]{0,1:T(8,128)(2,1)S(1)} %bitcast.94, bf16[256,2048]{1,0:T(8,128)(2,1)} %param.35), kind=kOutput, calls=%fused_computation.162 | convolution fusion | flops 1073741824 | bytes 9961472 | tf_op jit(solution)/shard_map/dot_general | solution.py:172
  136.1 51.5 %reduce-scatter.3.cloned.1.call-done = f32[128,2048]{1,0:T(8,128)} async-done(((f32[1024,2048]{1,0:T(8,128)}), f32[128,2048]{1,0:T(8,128)}) %reduce-scatter.3.cloned.1.call-update) | async-done | bytes 1048592 | tf_op jit(solution)/shard_map/reduce_scatter | solution.py:171
  187.7 1.5 fusion.17
  190.4 71.2 %all-gather.6.cloned.1.call-done = bf16[2048,2048]{1,0:T(8,128)(2,1)} async-done(((bf16[128,2048]{1,0:T(8,128)(2,1)}), bf16[2048,2048]{1,0:T(8,128)(2,1)}) %all-gather.6.cloned.1.call-update) | async-done | bytes 8388624 | tf_op jit(solution)/shard_map/all_gather | solution.py:179
  261.5 10.1 %fusion.90 = f32[2048,384]{1,0:T(8,128)} fusion(bf16[2048,2048]{1,0:T(8,128)(2,1)} %all-gather.6.cloned.1.call-done, bf16[2048,384]{1,0:T(8,128)(2,1)} %param.37), kind=kOutput, calls=%fused_computation.163 | convolution fusion | flops 3221225472 | bytes 13107200 | tf_op jit(solution)/shard_map/dot_general | solution.py:180
  271.6 15.4 %fusion.10 = f32[2048,2048]{1,0:T(8,128)} fusion(bf16[384,2048]{1,0:T(8,128)(2,1)S(1)} %copy-done, f32[2048,384]{1,0:T(8,128)} %fusion.90, bf16[2048,2048]{1,0:T(8,128)(2,1)} %all-gather.6.cloned.1.call-done, bf16[2048,384]{1,0:T(8,128)(2,1)} %param.38), kind=kOutput, calls=%fused_computation.26 | convolution fusion | flops 6447169536 | bytes 31457280 | tf_op jit(solution)/shard_map/dot_general | solution.py:184
  287.0 110.1 %reduce-scatter.5.cloned.1.call-done = f32[128,2048]{1,0:T(8,128)} async-done(((f32[2048,2048]{1,0:T(8,128)}), f32[128,2048]{1,0:T(8,128)}) %reduce-scatter.5.cloned.1.call-update) | async-done | bytes 1048592 | tf_op jit(solution)/shard_map/reduce_scatter | solution.py:183
  398.6 1.5 scatter_custom_fusion
  402.4 23.1 %psum.7 = bf16[9,2048]{1,0:T(8,128)(2,1)S(1)} all-reduce(bf16[9,2048]{1,0:T(8,128)(2,1)S(1)} %fusion.48), channel_id=1, replica_groups=mesh['req'=16,'kv'=8] {'kv'}, use_global_device_ids=true, to_apply=%region_16.17 | all-reduce | flops 18432 | bytes 73728 | tf_op jit(solution)/shard_map/psum | solution.py:12
  425.5 8.6 %all-to-all-start.1 = ((bf16[128,2,1024]{2,1,0:T(2,128)(2,1)}), bf16[128,2,1024]{2,1,0:T(2,128)(2,1)S(1)}, u32[]{:S(2)}, u32[]{:S(2)}) async-start(bf16[128,2,1024]{2,1,0:T(2,128)(2,1)} %reshape.486), calls=%async_computation.3 | async-start | bytes 1048576 | tf_op jit(solution)/shard_map/all_to_all | solution.py:77
  434.1 22.4 %all-gather = bf16[16,9,2048]{2,1,0:T(8,128)(2,1)S(1)} all-gather(bf16[1,9,2048]{2,1,0:T(8,128)(2,1)S(1)} %bitcast.99), channel_id=1, replica_groups=mesh['req'=16,'kv'=8] {'req'}, dimensions={0}, use_global_device_ids=true | all-gather | bytes 626688 | tf_op jit(solution)/shard_map/all_gather | solution.py:197
  457.5 4.4 convolution_reduce_fusion
  461.9 68.8 %pmax.7 = f32[144]{0:T(256)} all-reduce(f32[144]{0:T(256)S(1)} %convolution_reduce_fusion), channel_id=1, replica_groups=mesh['req'=16,'kv'=8] {'req','kv'}, use_global_device_ids=true, to_apply=%region_18.19 | all-reduce | flops 144 | bytes 1152 | tf_op jit(solution)/shard_map/pmax | solution.py:203
  531.1 2.4 scatter_custom_fusion.1
  (102 shorter events, 23.8 us)
Async XLA Ops:
  7.2 264.4 %copy-start = (bf16[384,2048]{1,0:T(8,128)(2,1)S(1)}, bf16[384,2048]{1,0:T(8,128)(2,1)}, u32[]{:S(2)}) copy-start(bf16[384,2048]{1,0:T(8,128)(2,1)} %param.39) | copy-start | bytes 4718596
  7.2 12.8 %copy-start.1 = (bf16[128,2048]{1,0:T(8,128)(2,1)S(1)}, bf16[128,2048]{1,0:T(8,128)(2,1)}, u32[]{:S(2)}) copy-start(bf16[128,2048]{1,0:T(8,128)(2,1)} %param.21) | copy-start | bytes 1572868
  7.2 8.5 %sort.19.cloned.1.call-start = ((), (), s32[]{:S(2)}) async-start(), calls=%async_computation.8 | async-start | bytes 393248 | tf_op jit(solution)/shard_map/jit(argsort)/sort | solution.py:111
  23.6 25.2 %all-to-all-start = ((bf16[128,2,1024]{2,1,0:T(2,128)(2,1)}), bf16[128,2,1024]{2,1,0:T(2,128)(2,1)S(1)}, u32[]{:S(2)}, u32[]{:S(2)}) async-start(bf16[128,2,1024]{2,1,0:T(2,128)(2,1)} %reshape.484), calls=%async_computation | async-start | bytes 1048576 | tf_op jit(solution)/shard_map/all_to_all | solution.py:77
  35.1 48.0 %all-gather.4.cloned.1.call-start = ((), (), s32[]{:S(2)}) async-start(), calls=%async_computation.4 | async-start | bytes 4718592 | tf_op jit(solution)/shard_map/all_gather | solution.py:128
  35.9 17.4 %copy-start.6 = (f32[2048]{0:T(1024)S(1)}, f32[2048]{0:T(1024)}, u32[]{:S(2)}) copy-start(f32[2048]{0:T(1024)} %param.29) | copy-start | bytes 24580
  50.6 4.7 copy-start.9
  53.1 30.1 %copy-start.13 = (bf16[2048,128]{1,0:T(8,128)(2,1)S(1)}, bf16[2048,128]{1,0:T(8,128)(2,1)}, u32[]{:S(2)}) copy-start(bf16[2048,128]{1,0:T(8,128)(2,1)} %param.32) | copy-start | bytes 1572868
  54.3 133.4 %reduce-scatter.3.cloned.1.call-start = ((), (), s32[]{:S(2)}) async-start(), calls=%async_computation.5 | async-start | bytes 9437184 | tf_op jit(solution)/shard_map/reduce_scatter | solution.py:171
  62.7 24.8 %copy-start.4 = (bf16[2048,128]{1,0:T(8,128)(2,1)S(1)}, bf16[2048,128]{1,0:T(8,128)(2,1)}, u32[]{:S(2)}) copy-start(bf16[2048,128]{1,0:T(8,128)(2,1)} %param.31) | copy-start | bytes 1572868
  83.2 4.4 copy-start.3
  86.8 2.3 copy-start.10
  86.8 3.7 copy-start.12
  90.5 4.8 copy-start.11
  95.3 2.5 copy-start.2
  102.4 15.9 %copy-start.5 = (bf16[1016,128]{1,0:T(8,128)(2,1)S(1)}, bf16[1016,128]{1,0:T(8,128)(2,1)}, u32[]{:S(2)}) copy-start(bf16[1016,128]{1,0:T(8,128)(2,1)} %slice.58) | copy-start | bytes 780292
  136.1 53.1 %copy-start.7 = (f32[2048]{0:T(1024)S(1)}, f32[2048]{0:T(1024)}, u32[]{:S(2)}) copy-start(f32[2048]{0:T(1024)} %param.36) | copy-start | bytes 24580
  136.1 125.4 %all-gather.6.cloned.1.call-start = ((), (), s32[]{:S(2)}) async-start(), calls=%async_computation.6 | async-start | bytes 8912896 | tf_op jit(solution)/shard_map/all_gather | solution.py:179
  190.1 207.0 %reduce-scatter.5.cloned.1.call-start = ((), (), s32[]{:S(2)}) async-start(), calls=%async_computation.7 | async-start | bytes 17825792 | tf_op jit(solution)/shard_map/reduce_scatter | solution.py:183
  287.0 115.3 %copy-start.8 = (f32[2048]{0:T(1024)S(1)}, f32[2048]{0:T(1024)}, u32[]{:S(2)}) copy-start(f32[2048]{0:T(1024)} %param.40) | copy-start | bytes 24580
  425.5 105.2 %all-to-all-start.1 = ((bf16[128,2,1024]{2,1,0:T(2,128)(2,1)}), bf16[128,2,1024]{2,1,0:T(2,128)(2,1)S(1)}, u32[]{:S(2)}, u32[]{:S(2)}) async-start(bf16[128,2,1024]{2,1,0:T(2,128)(2,1)} %reshape.486), calls=%async_computation.3 | async-start | bytes 1048576 | tf_op jit(solution)/shard_map/all_to_all | solution.py:77
Sparse Core Ops, SparseCore 0:
  10.8 4.6 sort.21.cloned.1.call-done
  54.4 28.7 all-gather.3
  136.2 51.3 reduce-scatter.2
  190.4 71.0 all-gather.5
  287.1 109.9 reduce-scatter.4
  (1 shorter events, 0.0 us)
where the time goes:
time: 545 us; the launch traced here: 540 us
  waiting for transfers between devices  266 us (49%)
  blocking collectives  114 us (21%)
  matrix products  74.9 us (14%)
  local copies, waits for them, and re-layouts  25.5 us (5%)
  other arithmetic  23.6 us (4%)
  starting transfers between devices  20.7 us (4%)
  between operations  15 us (3%)
    reduce_scatter x1, waiting for transfers between devices, shards(): lax.psum_scatter(jnp.dot(hidden_act, w_down, preferred_element_type=jnp.f...  110 us
    all_gather x1, waiting for transfers between devices, shards(): rows_piece = lax.all_gather(ffn_in, 'req', axis=0, tiled=True)  71.2 us
    pmax x1, blocking collectives, shards(): max_logit = lax.pmax(local_peaks, ('req', 'kv'))  68.8 us
    reduce_scatter x1, waiting for transfers between devices, shards(): lax.psum_scatter(jnp.dot(attended, o_proj, preferred_element_type=jnp.flo...  51.5 us
    psum x1, blocking collectives, spread(): return lax.psum(jnp.where(mine, value, jnp.zeros_like(value)), axis)  23.1 us
    all_gather x1, blocking collectives, shards(): lax.all_gather(tail_rows, 'req', axis=0, tiled=True)  22.4 us
    all_gather x1, waiting for transfers between devices, shards(): rows_piece = lax.all_gather(normed, 'kv', axis=0, tiled=True)  20.4 us
    all_to_all x2, starting transfers between devices, regroup(): lax.all_to_all(rows_in, ('req', 'kv'), split_axis=0, concat_axis=0, tiled...  20.1 us
  transfers between devices with their start and end apart: 6, of which 5 were waited for; matrix products, arithmetic and copies ran while one was open for 3% of the time, Pallas kernels for 0%

commit v1 on v0

--- a/solution.py
+++ b/solution.py
@@ -5,6 +5,24 @@
 
 EPS = 1e-06
 NEG = -1e30
+
+
+def collect(value, axis, dim):
+    ways, here, step = (lax.axis_size(axis), lax.axis_index(axis), value.shape[dim])
+    shape = [n * ways if d == dim else n for d, n in enumerate(value.shape)]
+    full = lax.dynamic_update_slice_in_dim(
+        jnp.zeros(shape, value.dtype), value, here * step, axis=dim
+    )
+    going_up = going_down = value
+    for far in range(1, ways // 2 + 1):
+        going_up = lax.ppermute(going_up, axis, [(d, (d + 1) % ways) for d in range(ways)])
+        full = lax.dynamic_update_slice_in_dim(full, going_up, (here - far) % ways * step, axis=dim)
+        if 2 * far < ways:
+            going_down = lax.ppermute(going_down, axis, [(d, (d - 1) % ways) for d in range(ways)])
+            full = lax.dynamic_update_slice_in_dim(
+                full, going_down, (here + far) % ways * step, axis=dim
+            )
+    return full
 
 
 def spread(value, axis, root):
@@ -193,12 +211,7 @@
     tail_rows = norm_rows(out_rows[rows_dev - dec_count - 1 :], final_gain).astype(jnp.bfloat16)
     tail_rows = spread(tail_rows, "kv", kv_count - 1)
     local_peaks = jnp.max(
-        jnp.dot(
-            lax.all_gather(tail_rows, "req", axis=0, tiled=True),
-            lm_head,
-            preferred_element_type=jnp.float32,
-        ),
-        axis=1,
+        jnp.dot(collect(tail_rows, "req", 0), lm_head, preferred_element_type=jnp.float32), axis=1
     )
     max_logit = lax.pmax(local_peaks, ("req", "kv"))
     return (layer_out, max_logit)

time: 545 us -> 586 us (1.075)
  starting transfers between devices: 20.7 us -> 62.2 us
  blocking collectives: 114 us -> 89.5 us
  local copies, waits for them, and re-layouts: 25.5 us -> 38.2 us
  waiting for transfers between devices: 266 us -> 277 us
    ppermute x0 -> x15, starting transfers between devices: none -> 35.7 us  [the longest x7 34.1 us: collect(): lax.ppermute(going_down, axis, [(d, (d - 1) % ways) for d in range(ways)])]
    all_gather x1 -> x0, blocking collectives: 22.4 us -> none  [shards(): lax.all_gather(tail_rows, 'req', axis=0, tiled=True)]
    dynamic_update_slice x0 -> x16, local copies, waits for them, and re-layouts: none -> 12.1 us  [the longest x8 5.9 us: collect(): lax.dynamic_update_slice_in_dim(full, going_up, (here - far) % ways * ste...]
    ppermute x0 -> x15, waiting for transfers between devices: none -> 11.6 us  [the longest x8 7.6 us: collect(): lax.ppermute(going_up, axis, [(d, (d + 1) % ways) for d in range(ways)])]
  transfers between devices with their start and end apart: 6 -> 21, of which waited for: 5 -> 13; matrix products, arithmetic and copies ran while one was open for 3% -> 5% of each run, Pallas kernels for 0% -> 0%
where the time goes in v1:
time: 586 us; the launch traced here: 581 us
  waiting for transfers between devices  277 us (47%)
  blocking collectives  89.5 us (15%)
  matrix products  74.7 us (13%)
  starting transfers between devices  62.2 us (11%)
  local copies, waits for them, and re-layouts  38.2 us (7%)
  other arithmetic  24.1 us (4%)
  between operations  15.2 us (3%)
    reduce_scatter x1, waiting for transfers between devices, shards(): lax.psum_scatter(jnp.dot(hidden_act, w_down, preferred_element_type=jnp.f...  110 us
    all_gather x1, waiting for transfers between devices, shards(): rows_piece = lax.all_gather(ffn_in, 'req', axis=0, tiled=True)  71.2 us
    pmax x1, blocking collectives, shards(): max_logit = lax.pmax(local_peaks, ('req', 'kv'))  66.4 us
    reduce_scatter x1, waiting for transfers between devices, shards(): lax.psum_scatter(jnp.dot(attended, o_proj, preferred_element_type=jnp.flo...  51.5 us
    ppermute x7, starting transfers between devices, collect(): lax.ppermute(going_down, axis, [(d, (d - 1) % ways) for d in range(ways)])  34.1 us
    all_to_all x2, starting transfers between devices, regroup(): lax.all_to_all(rows_in, ('req', 'kv'), split_axis=0, concat_axis=0, tiled...  25.8 us
    psum x1, blocking collectives, spread(): return lax.psum(jnp.where(mine, value, jnp.zeros_like(value)), axis)  23.1 us
    all_gather x1, waiting for transfers between devices, shards(): rows_piece = lax.all_gather(normed, 'kv', axis=0, tiled=True)  20.4 us
  transfers between devices with their start and end apart: 21, of which 13 were waited for; matrix products, arithmetic and copies ran while one was open for 5% of the time, Pallas kernels for 0%

profile of v1, /device:TPU:1, one launch (start us, length us, event | category | flops | bytes accessed | tf_op | source)
XLA Modules:
  0.0 580.9 jit_solution(13785249885975179417)
XLA Ops:
  10.3 5.5 sort.19.cloned.1.call-done
  17.0 1.9 gather_fusion.2
  24.0 11.5 %all-to-all-start = ((bf16[128,2,1024]{2,1,0:T(2,128)(2,1)}), bf16[128,2,1024]{2,1,0:T(2,128)(2,1)S(1)}, u32[]{:S(2)}, u32[]{:S(2)}) async-start(bf16[128,2,1024]{2,1,0:T(2,128)(2,1)} %reshape.482), calls=%async_computation | async-start | bytes 1048576 | tf_op jit(solution)/shard_map/all_to_all | solution.py:95
  37.1 12.1 %all-to-all-done = bf16[128,2,1024]{2,1,0:T(2,128)(2,1)S(1)} async-done(((bf16[128,2,1024]{2,1,0:T(2,128)(2,1)}), bf16[128,2,1024]{2,1,0:T(2,128)(2,1)S(1)}, u32[]{:S(2)}, u32[]{:S(2)}) %all-to-all-start) | async-done | bytes 524320 | tf_op jit(solution)/shard_map/all_to_all | solution.py:95
  55.8 3.1 multiply_cosine_fusion
  59.0 4.2 fusion.4
  63.2 20.4 %all-gather.3.cloned.1.call-done = bf16[1024,2048]{1,0:T(8,128)(2,1)} async-done(((bf16[128,2048]{1,0:T(8,128)(2,1)}), bf16[1024,2048]{1,0:T(8,128)(2,1)}) %all-gather.3.cloned.1.call-update) | async-done | bytes 4194320 | tf_op jit(solution)/shard_map/all_gather | solution.py:146
  83.6 3.9 multiply_reduce_fusion.1
  90.8 2.3 multiply_reduce_fusion
  100.3 2.9 fusion.43
  103.3 15.9 %fusion.84 = (f32[2,1016]{1,0:T(2,128)S(1)}, f32[2,1016,3064]{2,1,0:T(8,128)}) fusion(pred[1016,3064]{1,0:T(8,128)(4,1)} %fusion.4, bf16[1016,128]{1,0:T(8,128)(2,1)} %copy.80, bf16[2048,128]{1,0:T(8,128)(2,1)} %bitcast.101, bf16[1024,2,64]{2,0,1:T(8,128)(2,1)S(1)} %get-tuple-element.6, bf16[1024,2,64]{2,0,1:T(8,128)(2,1)S(1)} %get-tuple-element.7), kind=kOutput, calls=%fused_computation.161 | convolution fusion | flops 1621384704 | bytes 29334016 | tf_op jit(solution)/shard_map/sub | solution.py:66
  119.2 11.7 %fusion.12 = bf16[1016,2,128]{2,0,1:T(8,128)(2,1)S(1)} fusion(f32[2,1016,3064]{2,1,0:T(8,128)} %get-tuple-element.21, f32[2,1016]{1,0:T(2,128)S(1)} %get-tuple-element.20, bf16[1016,128]{1,0:T(8,128)(2,1)S(1)} %slice-done, bf16[2048,128]{1,0:T(8,128)(2,1)} %bitcast.102), kind=kOutput, calls=%fused_computation.28 | convolution fusion | flops 1608149248 | bytes 26216896 | tf_op jit(solution)/shard_map/gck,kd->cgd/dot_general | solution.py:68
  131.2 5.7 fusion.89
  137.0 51.5 %reduce-scatter.3.cloned.1.call-done = f32[128,2048]{1,0:T(8,128)} async-done(((f32[1024,2048]{1,0:T(8,128)}), f32[128,2048]{1,0:T(8,128)}) %reduce-scatter.3.cloned.1.call-update) | async-done | bytes 1048592 | tf_op jit(solution)/shard_map/reduce_scatter | solution.py:189
  191.2 71.2 %all-gather.5.cloned.1.call-done = bf16[2048,2048]{1,0:T(8,128)(2,1)} async-done(((bf16[128,2048]{1,0:T(8,128)(2,1)}), bf16[2048,2048]{1,0:T(8,128)(2,1)}) %all-gather.5.cloned.1.call-update) | async-done | bytes 8388624 | tf_op jit(solution)/shard_map/all_gather | solution.py:197
  262.4 10.1 %fusion.90 = f32[2048,384]{1,0:T(8,128)} fusion(bf16[2048,2048]{1,0:T(8,128)(2,1)} %all-gather.5.cloned.1.call-done, bf16[2048,384]{1,0:T(8,128)(2,1)} %param.37), kind=kOutput, calls=%fused_computation.163 | convolution fusion | flops 3221225472 | bytes 13107200 | tf_op jit(solution)/shard_map/dot_general | solution.py:198
  272.5 15.4 %fusion.10 = f32[2048,2048]{1,0:T(8,128)} fusion(bf16[384,2048]{1,0:T(8,128)(2,1)S(1)} %copy-done, f32[2048,384]{1,0:T(8,128)} %fusion.90, bf16[2048,2048]{1,0:T(8,128)(2,1)} %all-gather.5.cloned.1.call-done, bf16[2048,384]{1,0:T(8,128)(2,1)} %param.38), kind=kOutput, calls=%fused_computation.26 | convolution fusion | flops 6447169536 | bytes 31457280 | tf_op jit(solution)/shard_map/dot_general | solution.py:202
  287.9 110.1 %reduce-scatter.5.cloned.1.call-done = f32[128,2048]{1,0:T(8,128)} async-done(((f32[2048,2048]{1,0:T(8,128)}), f32[128,2048]{1,0:T(8,128)}) %reduce-scatter.5.cloned.1.call-update) | async-done | bytes 1048592 | tf_op jit(solution)/shard_map/reduce_scatter | solution.py:201
  399.6 23.1 %psum.7 = bf16[9,2048]{1,0:T(8,128)(2,1)S(1)} all-reduce(bf16[9,2048]{1,0:T(8,128)(2,1)S(1)} %fusion.48), channel_id=1, replica_groups=mesh['req'=16,'kv'=8] {'kv'}, use_global_device_ids=true, to_apply=%region_16.17 | all-reduce | flops 18432 | bytes 73728 | tf_op jit(solution)/shard_map/psum | solution.py:30
  424.2 3.3 collective-permute-start.1
  429.2 4.8 collective-permute-start.3
  435.6 4.8 collective-permute-start.5
  442.1 4.9 collective-permute-start.7
  447.0 2.3 collective-permute-done.6
  453.1 14.3 %all-to-all-start.1 = ((bf16[128,2,1024]{2,1,0:T(2,128)(2,1)}), bf16[128,2,1024]{2,1,0:T(2,128)(2,1)S(1)}, u32[]{:S(2)}, u32[]{:S(2)}) async-start(bf16[128,2,1024]{2,1,0:T(2,128)(2,1)} %reshape.484), calls=%async_computation.3 | async-start | bytes 1048576 | tf_op jit(solution)/shard_map/all_to_all | solution.py:95
  467.5 5.6 collective-permute-start.9
  473.1 2.9 collective-permute-done.9
  476.0 5.6 collective-permute-start.11
  483.0 5.1 collective-permute-start.13
  500.6 4.2 convolution_reduce_fusion
  504.8 66.4 %pmax.7 = f32[144]{0:T(256)} all-reduce(f32[144]{0:T(256)S(1)} %convolution_reduce_fusion), channel_id=1, replica_groups=mesh['req'=16,'kv'=8] {'req','kv'}, use_global_device_ids=true, to_apply=%region_18.19 | all-reduce | flops 144 | bytes 1152 | tf_op jit(solution)/shard_map/pmax | solution.py:216
  571.7 2.5 scatter_custom_fusion.1
  (156 shorter events, 56.5 us)
Async XLA Ops:
  7.2 265.3 %copy-start = (bf16[384,2048]{1,0:T(8,128)(2,1)S(1)}, bf16[384,2048]{1,0:T(8,128)(2,1)}, u32[]{:S(2)}) copy-start(bf16[384,2048]{1,0:T(8,128)(2,1)} %param.39) | copy-start | bytes 4718596
  7.2 13.4 %copy-start.1 = (bf16[128,2048]{1,0:T(8,128)(2,1)S(1)}, bf16[128,2048]{1,0:T(8,128)(2,1)}, u32[]{:S(2)}) copy-start(bf16[128,2048]{1,0:T(8,128)(2,1)} %param.21) | copy-start | bytes 1572868
  7.2 8.5 %sort.19.cloned.1.call-start = ((), (), s32[]{:S(2)}) async-start(), calls=%async_computation.8 | async-start | bytes 393248 | tf_op jit(solution)/shard_map/jit(argsort)/sort | solution.py:129
  24.0 25.2 %all-to-all-start = ((bf16[128,2,1024]{2,1,0:T(2,128)(2,1)}), bf16[128,2,1024]{2,1,0:T(2,128)(2,1)S(1)}, u32[]{:S(2)}, u32[]{:S(2)}) async-start(bf16[128,2,1024]{2,1,0:T(2,128)(2,1)} %reshape.482), calls=%async_computation | async-start | bytes 1048576 | tf_op jit(solution)/shard_map/all_to_all | solution.py:95
  35.5 48.0 %all-gather.3.cloned.1.call-start = ((), (), s32[]{:S(2)}) async-start(), calls=%async_computation.4 | async-start | bytes 4718592 | tf_op jit(solution)/shard_map/all_gather | solution.py:146
  37.1 12.2 %copy-start.12 = (s32[128]{0:T(128)}, s32[128]{0:T(128)S(1)}, u32[]{:S(2)}) copy-start(s32[128]{0:T(128)S(1)} %fusion.50) | copy-start | bytes 1540
  37.1 16.6 %copy-start.7 = (f32[2048]{0:T(1024)S(1)}, f32[2048]{0:T(1024)}, u32[]{:S(2)}) copy-start(f32[2048]{0:T(1024)} %param.29) | copy-start | bytes 24580
  53.5 30.1 %copy-start.4 = (bf16[2048,128]{1,0:T(8,128)(2,1)S(1)}, bf16[2048,128]{1,0:T(8,128)(2,1)}, u32[]{:S(2)}) copy-start(bf16[2048,128]{1,0:T(8,128)(2,1)} %param.31) | copy-start | bytes 1572868
  54.7 133.8 %reduce-scatter.3.cloned.1.call-start = ((), (), s32[]{:S(2)}) async-start(), calls=%async_computation.5 | async-start | bytes 9437184 | tf_op jit(solution)/shard_map/reduce_scatter | solution.py:189
  59.0 28.5 %copy-start.14 = (f32[128]{0:T(128)S(1)}, f32[128]{0:T(128)}, u32[]{:S(2)}) copy-start(f32[128]{0:T(128)} %param.34) | copy-start | bytes 1540
  83.6 5.3 copy-start.17
  103.3 15.9 %slice-start = ((bf16[1024,128]{1,0:T(8,128)(2,1)}), bf16[1016,128]{1,0:T(8,128)(2,1)S(1)}, s32[]{:S(2)}) async-start(bf16[1024,128]{1,0:T(8,128)(2,1)} %copy-done.5), calls=%async_computation.10 | async-start | bytes 520192 | tf_op jit(solution)/shard_map/slice | solution.py:176
  136.9 53.1 %copy-start.8 = (f32[2048]{0:T(1024)S(1)}, f32[2048]{0:T(1024)}, u32[]{:S(2)}) copy-start(f32[2048]{0:T(1024)} %param.36) | copy-start | bytes 24580
  137.0 125.4 %all-gather.5.cloned.1.call-start = ((), (), s32[]{:S(2)}) async-start(), calls=%async_computation.6 | async-start | bytes 8912896 | tf_op jit(solution)/shard_map/all_gather | solution.py:197
  191.0 207.0 %reduce-scatter.5.cloned.1.call-start = ((), (), s32[]{:S(2)}) async-start(), calls=%async_computation.7 | async-start | bytes 17825792 | tf_op jit(solution)/shard_map/reduce_scatter | solution.py:201
  287.9 111.6 %copy-start.9 = (f32[2048]{0:T(1024)S(1)}, f32[2048]{0:T(1024)}, u32[]{:S(2)}) copy-start(f32[2048]{0:T(1024)} %param.40) | copy-start | bytes 24580
  422.7 6.5 %collective-permute-start = (bf16[9,2048]{1,0:T(8,128)(2,1)S(1)}, bf16[9,2048]{1,0:T(8,128)(2,1)S(1)}, u32[]{:S(2)}, u32[]{:S(2)}) collective-permute-start(bf16[9,2048]{1,0:T(8,128)(2,1)S(1)} %psum.7), channel_id=1, source_target_pairs={{0,8},{8,16},{16,24},{24,32},{32,40},{40,48},{48,56},{56,64},{64,7... | collective-permute-start | bytes 110600 | tf_op jit(solution)/shard_map/ppermute | solution.py:18
  424.2 5.0 collective-permute-start.1
  429.2 6.4 %collective-permute-start.2 = (bf16[9,2048]{1,0:T(8,128)(2,1)S(1)}, bf16[9,2048]{1,0:T(8,128)(2,1)S(1)}, u32[]{:S(2)}, u32[]{:S(2)}) collective-permute-start(bf16[9,2048]{1,0:T(8,128)(2,1)S(1)} %collective-permute-done), channel_id=1, source_target_pairs={{0,8},{8,16},{16,24},{24,32},{32,40},{40,48},{48,56},{56,64},{64,7... | collective-permute-start | bytes 110600 | tf_op jit(solution)/shard_map/ppermute | solution.py:18
  429.2 6.4 %collective-permute-start.3 = (bf16[9,2048]{1,0:T(8,128)(2,1)S(1)}, bf16[9,2048]{1,0:T(8,128)(2,1)S(1)}, u32[]{:S(2)}, u32[]{:S(2)}) collective-permute-start(bf16[9,2048]{1,0:T(8,128)(2,1)S(1)} %collective-permute-done.1), channel_id=1, source_target_pairs={{0,120},{8,0},{16,8},{24,16},{32,24},{40,32},{48,40},{56,48},{64,5... | collective-permute-start | bytes 110600 | tf_op jit(solution)/shard_map/ppermute | solution.py:21
  435.6 6.4 %collective-permute-start.4 = (bf16[9,2048]{1,0:T(8,128)(2,1)S(1)}, bf16[9,2048]{1,0:T(8,128)(2,1)S(1)}, u32[]{:S(2)}, u32[]{:S(2)}) collective-permute-start(bf16[9,2048]{1,0:T(8,128)(2,1)S(1)} %collective-permute-done.2), channel_id=1, source_target_pairs={{0,8},{8,16},{16,24},{24,32},{32,40},{40,48},{48,56},{56,64},{64,7... | collective-permute-start | bytes 110600 | tf_op jit(solution)/shard_map/ppermute | solution.py:18
  435.6 6.4 %collective-permute-start.5 = (bf16[9,2048]{1,0:T(8,128)(2,1)S(1)}, bf16[9,2048]{1,0:T(8,128)(2,1)}, u32[]{:S(2)}, u32[]{:S(2)}) collective-permute-start(bf16[9,2048]{1,0:T(8,128)(2,1)S(1)} %collective-permute-done.3), channel_id=1, source_target_pairs={{0,120},{8,0},{16,8},{24,16},{32,24},{40,32},{48,40},{56,48},{64,5... | collective-permute-start | bytes 110600 | tf_op jit(solution)/shard_map/ppermute | solution.py:21
  442.1 7.2 %collective-permute-start.6 = (bf16[9,2048]{1,0:T(8,128)(2,1)S(1)}, bf16[9,2048]{1,0:T(8,128)(2,1)}, u32[]{:S(2)}, u32[]{:S(2)}) collective-permute-start(bf16[9,2048]{1,0:T(8,128)(2,1)S(1)} %collective-permute-done.4), channel_id=1, source_target_pairs={{0,8},{8,16},{16,24},{24,32},{32,40},{40,48},{48,56},{56,64},{64,7... | collective-permute-start | bytes 110600 | tf_op jit(solution)/shard_map/ppermute | solution.py:18
  442.1 25.4 %collective-permute-start.7 = (bf16[9,2048]{1,0:T(8,128)(2,1)}, bf16[9,2048]{1,0:T(8,128)(2,1)}, u32[]{:S(2)}, u32[]{:S(2)}) collective-permute-start(bf16[9,2048]{1,0:T(8,128)(2,1)} %collective-permute-done.5), channel_id=1, source_target_pairs={{0,120},{8,0},{16,8},{24,16},{32,24},{40,32},{48,40},{56,48},{64,5... | collective-permute-start | bytes 110600 | tf_op jit(solution)/shard_map/ppermute | solution.py:21
  449.2 23.9 %collective-permute-start.8 = (bf16[9,2048]{1,0:T(8,128)(2,1)}, bf16[9,2048]{1,0:T(8,128)(2,1)}, u32[]{:S(2)}, u32[]{:S(2)}) collective-permute-start(bf16[9,2048]{1,0:T(8,128)(2,1)} %collective-permute-done.6), channel_id=1, source_target_pairs={{0,8},{8,16},{16,24},{24,32},{32,40},{40,48},{48,56},{56,64},{64,7... | collective-permute-start | bytes 110600 | tf_op jit(solution)/shard_map/ppermute | solution.py:18
  453.1 118.1 %all-to-all-start.1 = ((bf16[128,2,1024]{2,1,0:T(2,128)(2,1)}), bf16[128,2,1024]{2,1,0:T(2,128)(2,1)S(1)}, u32[]{:S(2)}, u32[]{:S(2)}) async-start(bf16[128,2,1024]{2,1,0:T(2,128)(2,1)} %reshape.484), calls=%async_computation.3 | async-start | bytes 1048576 | tf_op jit(solution)/shard_map/all_to_all | solution.py:95
  467.5 8.5 %collective-permute-start.9 = (bf16[9,2048]{1,0:T(8,128)(2,1)}, bf16[9,2048]{1,0:T(8,128)(2,1)S(1)}, u32[]{:S(2)}, u32[]{:S(2)}) collective-permute-start(bf16[9,2048]{1,0:T(8,128)(2,1)} %collective-permute-done.7), channel_id=1, source_target_pairs={{0,120},{8,0},{16,8},{24,16},{32,24},{40,32},{48,40},{56,48},{64,5... | collective-permute-start | bytes 110600 | tf_op jit(solution)/shard_map/ppermute | solution.py:21
  473.1 8.7 %collective-permute-start.10 = (bf16[9,2048]{1,0:T(8,128)(2,1)}, bf16[9,2048]{1,0:T(8,128)(2,1)S(1)}, u32[]{:S(2)}, u32[]{:S(2)}) collective-permute-start(bf16[9,2048]{1,0:T(8,128)(2,1)} %collective-permute-done.8), channel_id=1, source_target_pairs={{0,8},{8,16},{16,24},{24,32},{32,40},{40,48},{48,56},{56,64},{64,7... | collective-permute-start | bytes 110600 | tf_op jit(solution)/shard_map/ppermute | solution.py:18
  476.0 6.9 %collective-permute-start.11 = (bf16[9,2048]{1,0:T(8,128)(2,1)S(1)}, bf16[9,2048]{1,0:T(8,128)(2,1)S(1)}, u32[]{:S(2)}, u32[]{:S(2)}) collective-permute-start(bf16[9,2048]{1,0:T(8,128)(2,1)S(1)} %collective-permute-done.9), channel_id=1, source_target_pairs={{0,120},{8,0},{16,8},{24,16},{32,24},{40,32},{48,40},{56,48},{64,5... | collective-permute-start | bytes 110600 | tf_op jit(solution)/shard_map/ppermute | solution.py:21
  481.8 6.4 %collective-permute-start.12 = (bf16[9,2048]{1,0:T(8,128)(2,1)S(1)}, bf16[9,2048]{1,0:T(8,128)(2,1)S(1)}, u32[]{:S(2)}, u32[]{:S(2)}) collective-permute-start(bf16[9,2048]{1,0:T(8,128)(2,1)S(1)} %collective-permute-done.10), channel_id=1, source_target_pairs={{0,8},{8,16},{16,24},{24,32},{32,40},{40,48},{48,56},{56,64},{64,7... | collective-permute-start | bytes 110600 | tf_op jit(solution)/shard_map/ppermute | solution.py:18
  483.0 16.4 %collective-permute-start.13 = (bf16[9,2048]{1,0:T(8,128)(2,1)S(1)}, bf16[9,2048]{1,0:T(8,128)(2,1)S(1)}, u32[]{:S(2)}, u32[]{:S(2)}) collective-permute-start(bf16[9,2048]{1,0:T(8,128)(2,1)S(1)} %collective-permute-done.11), channel_id=1, source_target_pairs={{0,120},{8,0},{16,8},{24,16},{32,24},{40,32},{48,40},{56,48},{64,5... | collective-permute-start | bytes 110600 | tf_op jit(solution)/shard_map/ppermute | solution.py:21
  488.3 11.7 %collective-permute-start.14 = (bf16[9,2048]{1,0:T(8,128)(2,1)S(1)}, bf16[9,2048]{1,0:T(8,128)(2,1)S(1)}, u32[]{:S(2)}, u32[]{:S(2)}) collective-permute-start(bf16[9,2048]{1,0:T(8,128)(2,1)S(1)} %collective-permute-done.12), channel_id=1, source_target_pairs={{0,8},{8,16},{16,24},{24,32},{32,40},{40,48},{48,56},{56,64},{64,7... | collective-permute-start | bytes 110600 | tf_op jit(solution)/shard_map/ppermute | solution.py:18
  (9 other events, 31.6 us)
Sparse Core Ops, SparseCore 0:
  10.8 4.6 sort.21.cloned.1.call-done
  54.8 28.7 all-gather.2
  137.1 51.3 reduce-scatter.2
  191.3 71.0 all-gather.4
  288.0 109.9 reduce-scatter.4
  (1 shorter events, 0.0 us)
